TPU v7x, 256 devices: a whole 4x4x8 slice. The times are simulated.
256 devices in a mesh: slab: 4 (over z_hi, core), row: 64 (over z_lo, x, y).
Axes of the slice: x: 4, y: 4, z: 8 (z_hi: 2, z_lo: 4; z = z_hi * 4 + z_lo), core: 2. Of those that a mesh axis runs over, the one named last changes fastest.
Arguments:
- rhs: bfloat16 [3, 2, 64, 8192], P(None, None, None, 'row'), may hold values from -6 to 6
- operator: bfloat16 [4, 2, 8192, 8192], P('slab', None, 'row'), may hold values from -0.046875 to 0.046875
- sources: bfloat16 [4, 3, 2, 64, 8192], P('slab', None, None, None, 'row'), may hold values from -6 to 6
- skeleton: int32 [4, 8192], P('slab'), may hold values from 0 to 8191, each once within a row
Outputs:
- outgoing: bfloat16 [4, 3, 2, 64, 8192], P('slab', None, None, None, 'row')
Inputs may be any that keep to these rules, and one draw needn't show every extreme that they name: Each row of skeleton is a permutation of 0 to 8191.
All inputs are finite; a program needn't handle non-finite values.
Results may differ from a plain program's by a relative error of at most 0.0055.
Values may be sent and summed in bfloat16 or wider, within the bound.
No kernel may reach another device: no remote copies, remote signals or barrier semaphores. Data moves between devices by JAX's collectives and lax.ppermute only.
A program may use at most 64 MiB of HBM per device.

v0:
```python
import jax
import jax.numpy as jnp
from jax import lax
from jax.experimental import pallas as pl
from jax.experimental.pallas import tpu as pltpu
from jax.sharding import PartitionSpec as P


AXES = ("slab", "row")
LANES = 128


def along(parity, v):
    high, gray = v >> 1, (v ^ (v >> 1)) & 1
    return (high, gray) if parity == 0 else (gray, high)


def inverse_along(parity, group, member):
    return next(v for v in range(4) if along(parity, v) == (group, member))


def place(parity, row):
    z, x, y = row >> 4, row >> 2 & 3, row & 3
    (gx, mx), (gy, my) = along(parity, x), along(parity, y)
    return z << 2 | gx << 1 | gy, mx << 1 | my


def row_of(parity, group, member):
    z = group >> 2
    x = inverse_along(parity, group >> 1 & 1, member >> 1)
    y = inverse_along(parity, group & 1, member & 1)
    return z << 4 | x << 2 | y


def exchange(value, target):
    pairs = []
    for source in range(256):
        half, core, row = source >> 7, source >> 6 & 1, source & 63
        half, core, row = target(half, core, row)
        pairs.append((source, half << 7 | core << 6 | row))
    return lax.ppermute(value, AXES, pairs)


def to_group(parity, mask):
    def target(half, core, row):
        group, member = place(parity, row)
        return half, core, row_of(parity, group ^ mask, member)

    return target


def to_member(parity, mask):
    def target(half, core, row):
        of = core if parity is None else parity
        group, member = place(of, row)
        return half, core, row_of(of, group, member ^ mask)

    return target


def other_core(half, core, row):
    return half, core ^ 1, row


def other_half(half, core, row):
    return half ^ 1, core, row ^ 2 << 4


def reorder_kernel(slot_ref, m_ref, *refs):
    outs, turned, placed = refs[:4], refs[4:6], refs[6]
    blocks = m_ref.shape[2] // LANES

    def turn(block, at):
        start = pl.multiple_of(block * LANES, LANES)
        for part in range(2):
            tile = m_ref[part, :, pl.ds(start, LANES)].astype(jnp.float32)
            turned[at][pl.ds(part, LANES, stride=2), :] = tile.T

    def put(block, at):
        slots = slot_ref.at[pl.ds(pl.multiple_of(block * LANES, LANES), LANES)]
        for r in range(LANES):
            to = pl.multiple_of(slots[r], 2)
            placed[pl.ds(to, 2), :] = turned[at][2 * r : 2 * r + 2, :]

    turn(0, 0)

    def body(pair, carry):
        turn(2 * pair + 1, 1)
        put(2 * pair, 0)
        turn(jnp.minimum(2 * pair + 2, blocks - 1), 0)
        put(2 * pair + 1, 1)
        return carry

    lax.fori_loop(0, blocks // 2, body, 0)
    rows = outs[0].shape[0]
    step = 256
    for at, out in enumerate(outs):

        def convert(n, carry, at=at, out=out):
            start = pl.multiple_of(n * step, step)
            base = 2 * (at * rows + start)
            for part in range(2):
                out[pl.ds(start, step), part * LANES : (part + 1) * LANES] = placed[
                    pl.ds(base + part, step, stride=2), :
                ].astype(out.dtype)
            return carry

        lax.fori_loop(0, rows // step, convert, 0)


def reorder(slots, matrix):
    columns = matrix.shape[2]
    vmem = pl.BlockSpec(memory_space=pltpu.VMEM)
    return pl.pallas_call(
        reorder_kernel,
        out_shape=[jax.ShapeDtypeStruct((columns // 4, 2 * LANES), jnp.bfloat16)] * 4,
        in_specs=[pl.BlockSpec(memory_space=pltpu.SMEM), vmem],
        out_specs=[vmem] * 4,
        scratch_shapes=[
            pltpu.VMEM((2 * LANES, LANES), jnp.float32),
            pltpu.VMEM((2 * LANES, LANES), jnp.float32),
            pltpu.VMEM((2 * columns, LANES), jnp.float32),
        ],
        cost_estimate=pl.CostEstimate(
            flops=0, bytes_accessed=40 * 1024 * 1024, transcendentals=0
        ),
        name="reorder",
    )(slots, matrix)


def product_kernel(own_ref, x0, x1, x2, x3, *refs):
    own, other, outs, joined = refs[:4], refs[4:8], refs[8:12], refs[12]
    use_own = own_ref[0] == 1
    width = joined.shape[0]
    for at, piece in enumerate((x0, x1, x2, x3)):
        for z in range(4):
            start = (z * 4 + at) * LANES
            joined[:, start : start + LANES] = piece[z * width : (z + 1) * width]
    half = width // 6

    for weights, wanted in ((own, use_own), (other, jnp.logical_not(use_own))):

        @pl.when(wanted)
        def _(weights=weights):
            for m in range(4):
                both = jnp.dot(
                    joined[...], weights[m][...], preferred_element_type=jnp.float32
                )
                both = both.reshape(3, 2, half, 2 * LANES)
                outs[m][:, 0] = both[:, 0, :, :LANES] - both[:, 1, :, LANES:]
                outs[m][:, 1] = both[:, 1, :, :LANES] + both[:, 0, :, LANES:]


def product(use_own, pieces, own, other):
    depth = own[0].shape[0]
    width = pieces[0].shape[0] // 4
    vmem = pl.BlockSpec(memory_space=pltpu.VMEM)
    return pl.pallas_call(
        product_kernel,
        out_shape=[jax.ShapeDtypeStruct((3, 2, width // 6, LANES), jnp.float32)] * 4,
        in_specs=[pl.BlockSpec(memory_space=pltpu.SMEM)] + [vmem] * 12,
        out_specs=[vmem] * 4,
        scratch_shapes=[pltpu.VMEM((width, depth), jnp.bfloat16)],
        compiler_params=pltpu.CompilerParams(vmem_limit_bytes=24 * 1024 * 1024),
        name="product",
    )(use_own, *pieces, *own, *other)


def gather(step, value):
    parity = step & 1
    flat = value.reshape(-1, LANES)
    parts = [flat] + [exchange(flat, to_group(parity, z << 2)) for z in (1, 2, 3)]
    joined = jnp.concatenate(parts, axis=0)
    return [joined] + [exchange(joined, to_group(parity, at)) for at in (1, 2, 3)]


def sweep(rhs, operator, sources, skeleton):
    slab, row = lax.axis_index("slab"), lax.axis_index("row")
    half, core = slab >> 1, slab & 1
    share = rhs.shape[2] // 2

    def placed(r):
        (g0, m0), (g1, m1) = place(0, r), place(1, r)
        return jnp.where(core == 0, g0, g1), jnp.where(core == 0, m0, m1)

    source = skeleton[0]
    from_row = source >> 7
    from_row = from_row ^ jnp.where(slab == 2, 2 << 4, 0)
    group, member = placed(from_row)
    my_group, my_member = placed(row)
    slots = (member ^ my_member) << 12 | (group ^ my_group) << 8 | (source & 127) << 1

    mine = lax.dynamic_slice_in_dim(rhs, core * share, share, 2)
    pieces = gather(0, mine)

    added_mine = lax.dynamic_slice_in_dim(sources[0], core * share, share, 2)
    added_sent = lax.dynamic_slice_in_dim(sources[0], (1 - core) * share, share, 2)
    added_other = exchange(added_sent, other_core)

    sent = reorder(slots, operator[0])
    own = [sent[0]] + [exchange(sent[m], to_member(None, m)) for m in (1, 2, 3)]
    other = [exchange(block, other_core) for block in own]

    values = []
    for step in range(4):
        parity = step & 1
        use_own = (core == parity).astype(jnp.int32).reshape(1)
        if step == 2:
            value = exchange(value, other_half)
        if step:
            pieces = gather(step, value)
        partial = product(use_own, pieces, own, other)
        total = partial[0]
        for m in (1, 2, 3):
            total = total + exchange(partial[m], to_member(parity, m))
        added = jnp.where(core == parity, added_mine, added_other)
        value = (total + added.astype(jnp.float32)).astype(jnp.bfloat16)
        values.append(value)
    first = jnp.where(half == 0, values[0], values[2])
    second = jnp.where(half == 0, values[1], values[3])
    kept = jnp.where(core == 0, first, second)
    arrived = exchange(jnp.where(core == 0, second, first), other_core)
    low = jnp.where(core == 0, kept, arrived)
    high = jnp.where(core == 0, arrived, kept)
    return jnp.concatenate([low, high], axis=2)[None]


def solution(mesh):
    return jax.shard_map(
        sweep,
        mesh=mesh,
        in_specs=(
            P(None, None, None, "row"),
            P("slab", None, "row", None),
            P("slab", None, None, None, "row"),
            P("slab", None),
        ),
        out_specs=P("slab", None, None, None, "row"),
        check_vma=False,
    )
```

profile of v0, /device:TPU:1, one launch (start us, length us, event | category | flops | bytes accessed | tf_op | source)
XLA Modules:
  0.0 206.6 jit_solution(8142280580347376294)
XLA Ops:
  1.6 12.1 %reorder.1 = (bf16[2048,256]{1,0:T(8,128)(2,1)}, bf16[2048,256]{1,0:T(8,128)(2,1)}, bf16[2048,256]{1,0:T(8,128)(2,1)}, bf16[2048,256]{1,0:T(8,128)(2,1)}) custom-call(s32[8192]{0:T(1024)} %fusion.10.slot_ref, bf16[2,128,8192]{2,1,0:T(8,128)(2,1)} %bitcast.27), custom_call_target="tpu_custom_call" | custom-call | bytes 41943040 | tf_op jit(solution)/shard_map/reorder/pallas_call | solution.py:114
  13.7 3.6 %collective-permute-start.6 = (bf16[2048,256]{1,0:T(8,128)(2,1)}, bf16[2048,256]{1,0:T(8,128)(2,1)S(1)}, u32[]{:S(2)}, u32[]{:S(2)}) collective-permute-start(bf16[2048,256]{1,0:T(8,128)(2,1)} %get-tuple-element.26), channel_id=1, source_target_pairs={{0,1},{1,0},{2,3},{3,2},{4,5},{5,4},{6,7},{7,6},{8,9},{9,8},{10,11... | collective-permute-start | bytes 3145736 | tf_op jit(solution)/shard_map/ppermute | solution.py:41
  17.3 2.5 %collective-permute-start.7 = (bf16[2048,256]{1,0:T(8,128)(2,1)}, bf16[2048,256]{1,0:T(8,128)(2,1)S(1)}, u32[]{:S(2)}, u32[]{:S(2)}) collective-permute-start(bf16[2048,256]{1,0:T(8,128)(2,1)} %get-tuple-element.27), channel_id=1, source_target_pairs={{0,4},{1,5},{2,6},{3,7},{4,0},{5,1},{6,2},{7,3},{8,12},{9,13},{10,... | collective-permute-start | bytes 3145736 | tf_op jit(solution)/shard_map/ppermute | solution.py:41
  20.4 9.3 %collective-permute-done.6.refs_1_ = bf16[2048,256]{1,0:T(8,128)(2,1)S(1)} collective-permute-done((bf16[2048,256]{1,0:T(8,128)(2,1)}, bf16[2048,256]{1,0:T(8,128)(2,1)S(1)}, u32[]{:S(2)}, u32[]{:S(2)}) %collective-permute-start.6) | collective-permute-done | bytes 1048608 | tf_op jit(solution)/shard_map/ppermute | solution.py:41
  29.6 2.3 %collective-permute-start.10 = (bf16[2048,256]{1,0:T(8,128)(2,1)S(1)}, bf16[2048,256]{1,0:T(8,128)(2,1)}, u32[]{:S(2)}, u32[]{:S(2)}) collective-permute-start(bf16[2048,256]{1,0:T(8,128)(2,1)S(1)} %collective-permute-done.6.refs_1_), channel_id=1, source_target_pairs={{0,64},{1,65},{2,66},{3,67},{4,68},{5,69},{6,70},{7,71},{8,72},{9,... | collective-permute-start | bytes 3145736 | tf_op jit(solution)/shard_map/ppermute | solution.py:41
  32.3 11.0 %collective-permute-done.8.refs_3_ = bf16[2048,256]{1,0:T(8,128)(2,1)S(1)} collective-permute-done((bf16[2048,256]{1,0:T(8,128)(2,1)}, bf16[2048,256]{1,0:T(8,128)(2,1)S(1)}, u32[]{:S(2)}, u32[]{:S(2)}) %collective-permute-start.8) | collective-permute-done | bytes 1048608 | tf_op jit(solution)/shard_map/ppermute | solution.py:41
  45.6 3.0 %collective-permute-start.2 = (bf16[192,128]{1,0:T(8,128)(2,1)S(1)}, bf16[192,128]{1,0:T(8,128)(2,1)S(1)}, u32[]{:S(2)}, u32[]{:S(2)}) collective-permute-start(bf16[192,128]{1,0:T(8,128)(2,1)S(1)} %bitcast.36), channel_id=1, source_target_pairs={{0,48},{1,49},{2,50},{3,51},{4,52},{5,53},{6,54},{7,55},{8,56},{9,... | collective-permute-start | bytes 147464 | tf_op jit(solution)/shard_map/ppermute | solution.py:41
  50.7 4.4 %collective-permute-done.1 = bf16[192,128]{1,0:T(8,128)(2,1)S(1)} collective-permute-done((bf16[192,128]{1,0:T(8,128)(2,1)S(1)}, bf16[192,128]{1,0:T(8,128)(2,1)S(1)}, u32[]{:S(2)}, u32[]{:S(2)}) %collective-permute-start.1) | collective-permute-done | bytes 49184 | tf_op jit(solution)/shard_map/ppermute | solution.py:41
  55.2 2.8 %collective-permute-done = bf16[192,128]{1,0:T(8,128)(2,1)S(1)} collective-permute-done((bf16[192,128]{1,0:T(8,128)(2,1)S(1)}, bf16[192,128]{1,0:T(8,128)(2,1)S(1)}, u32[]{:S(2)}, u32[]{:S(2)}) %collective-permute-start) | collective-permute-done | bytes 49184 | tf_op jit(solution)/shard_map/ppermute | solution.py:41
  58.0 3.8 %collective-permute-start.5 = (bf16[768,128]{1,0:T(8,128)(2,1)S(1)}, bf16[768,128]{1,0:T(8,128)(2,1)S(1)}, u32[]{:S(2)}, u32[]{:S(2)}) collective-permute-start(bf16[768,128]{1,0:T(8,128)(2,1)S(1)} %pad_maximum_fusion.x0), channel_id=1, source_target_pairs={{0,15},{1,14},{2,13},{3,12},{4,11},{5,10},{6,9},{7,8},{8,7},{9,6},... | collective-permute-start | bytes 589832 | tf_op jit(solution)/shard_map/ppermute | solution.py:41
  61.9 4.1 %collective-permute-done.5.x3 = bf16[768,128]{1,0:T(8,128)(2,1)S(1)} collective-permute-done((bf16[768,128]{1,0:T(8,128)(2,1)S(1)}, bf16[768,128]{1,0:T(8,128)(2,1)S(1)}, u32[]{:S(2)}, u32[]{:S(2)}) %collective-permute-start.5) | collective-permute-done | bytes 196640 | tf_op jit(solution)/shard_map/ppermute | solution.py:41
  68.0 4.4 %collective-permute-done.4.x2 = bf16[768,128]{1,0:T(8,128)(2,1)S(1)} collective-permute-done((bf16[768,128]{1,0:T(8,128)(2,1)S(1)}, bf16[768,128]{1,0:T(8,128)(2,1)S(1)}, u32[]{:S(2)}, u32[]{:S(2)}) %collective-permute-start.4) | collective-permute-done | bytes 196640 | tf_op jit(solution)/shard_map/ppermute | solution.py:41
  74.6 4.3 %collective-permute-done.3.x1 = bf16[768,128]{1,0:T(8,128)(2,1)} collective-permute-done((bf16[768,128]{1,0:T(8,128)(2,1)S(1)}, bf16[768,128]{1,0:T(8,128)(2,1)}, u32[]{:S(2)}, u32[]{:S(2)}) %collective-permute-start.3) | collective-permute-done | bytes 196640 | tf_op jit(solution)/shard_map/ppermute | solution.py:41
  83.2 3.5 %product.4 = (f32[3,2,32,128]{3,2,1,0:T(8,128)S(1)}, f32[3,2,32,128]{3,2,1,0:T(8,128)S(1)}, f32[3,2,32,128]{3,2,1,0:T(8,128)S(1)}, f32[3,2,32,128]{3,2,1,0:T(8,128)S(1)}) custom-call(s32[1]{0:T(128)} %bitcast.own_ref, bf16[768,128]{1,0:T(8,128)(2,1)S(1)} %pad_maximum_fusion.x0, bf16[768,128]{1,0:T(8,128)(2,1)} %collective-permute-done.3.x1, ...), custom_call_target="tpu_custom_call" | custom-call | tf_op jit(solution)/shard_map/product/pallas_call | solution.py:158
  86.9 2.5 %collective-permute-start.15 = (f32[3,2,32,128]{3,2,1,0:T(8,128)S(1)}, f32[3,2,32,128]{3,2,1,0:T(8,128)S(1)}, u32[]{:S(2)}, u32[]{:S(2)}) collective-permute-start(f32[3,2,32,128]{3,2,1,0:T(8,128)S(1)} %get-tuple-element.32), channel_id=1, source_target_pairs={{0,5},{1,4},{2,7},{3,6},{4,1},{5,0},{6,3},{7,2},{8,13},{9,12},{10,... | collective-permute-start | bytes 294920 | tf_op jit(solution)/shard_map/ppermute | solution.py:41
  89.5 6.9 %collective-permute-start.16 = (bf16[3,2,32,128]{3,2,1,0:T(8,128)(2,1)S(1)}, bf16[3,2,32,128]{3,2,1,0:T(8,128)(2,1)S(1)}, u32[]{:S(2)}, u32[]{:S(2)}) collective-permute-start(bf16[3,2,32,128]{3,2,1,0:T(8,128)(2,1)S(1)} %dynamic-slice_bitcast_fusion), channel_id=1, source_target_pairs={{0,64},{1,65},{2,66},{3,67},{4,68},{5,69},{6,70},{7,71},{8,72},{9,... | collective-permute-start | bytes 147464 | tf_op jit(solution)/shard_map/ppermute | solution.py:41
  97.4 3.7 %collective-permute-start.19 = (bf16[192,128]{1,0:T(8,128)(2,1)S(1)}, bf16[192,128]{1,0:T(8,128)(2,1)S(1)}, u32[]{:S(2)}, u32[]{:S(2)}) collective-permute-start(bf16[192,128]{1,0:T(8,128)(2,1)S(1)} %bitcast.28), channel_id=1, source_target_pairs={{0,48},{1,49},{2,50},{3,51},{4,52},{5,53},{6,54},{7,55},{8,56},{9,... | collective-permute-start | bytes 147464 | tf_op jit(solution)/shard_map/ppermute | solution.py:41
  102.6 2.8 %collective-permute-done.18 = bf16[192,128]{1,0:T(8,128)(2,1)S(1)} collective-permute-done((bf16[192,128]{1,0:T(8,128)(2,1)S(1)}, bf16[192,128]{1,0:T(8,128)(2,1)S(1)}, u32[]{:S(2)}, u32[]{:S(2)}) %collective-permute-start.18) | collective-permute-done | bytes 49184 | tf_op jit(solution)/shard_map/ppermute | solution.py:41
  108.2 3.0 %collective-permute-done.22.x3 = bf16[768,128]{1,0:T(8,128)(2,1)} collective-permute-done((bf16[768,128]{1,0:T(8,128)(2,1)S(1)}, bf16[768,128]{1,0:T(8,128)(2,1)}, u32[]{:S(2)}, u32[]{:S(2)}) %collective-permute-start.22) | collective-permute-done | bytes 196640 | tf_op jit(solution)/shard_map/ppermute | solution.py:41
  114.7 3.6 %product.5 = (f32[3,2,32,128]{3,2,1,0:T(8,128)S(1)}, f32[3,2,32,128]{3,2,1,0:T(8,128)S(1)}, f32[3,2,32,128]{3,2,1,0:T(8,128)S(1)}, f32[3,2,32,128]{3,2,1,0:T(8,128)S(1)}) custom-call(s32[1]{0:T(128)} %bitcast.9.own_ref, bf16[768,128]{1,0:T(8,128)(2,1)S(1)} %pad_maximum_fusion.1.x0, bf16[768,128]{1,0:T(8,128)(2,1)} %collective-permute-done.20.x1, ...), custom_call_target="tpu_custom_call" | custom-call | tf_op jit(solution)/shard_map/product/pallas_call | solution.py:158
  118.4 3.5 %collective-permute-start.23 = (f32[3,2,32,128]{3,2,1,0:T(8,128)S(1)}, f32[3,2,32,128]{3,2,1,0:T(8,128)S(1)}, u32[]{:S(2)}, u32[]{:S(2)}) collective-permute-start(f32[3,2,32,128]{3,2,1,0:T(8,128)S(1)} %get-tuple-element.34), channel_id=1, source_target_pairs={{0,3},{1,2},{2,1},{3,0},{4,7},{5,6},{6,5},{7,4},{8,11},{9,10},{10,... | collective-permute-start | bytes 294920 | tf_op jit(solution)/shard_map/ppermute | solution.py:41
  121.9 2.8 %collective-permute-start.24 = (f32[3,2,32,128]{3,2,1,0:T(8,128)S(1)}, f32[3,2,32,128]{3,2,1,0:T(8,128)S(1)}, u32[]{:S(2)}, u32[]{:S(2)}) collective-permute-start(f32[3,2,32,128]{3,2,1,0:T(8,128)S(1)} %get-tuple-element.35), channel_id=1, source_target_pairs={{0,12},{1,13},{2,14},{3,15},{4,8},{5,9},{6,10},{7,11},{8,4},{9,5},... | collective-permute-start | bytes 294920 | tf_op jit(solution)/shard_map/ppermute | solution.py:41
  126.7 5.3 %collective-permute-done.25 = f32[3,2,32,128]{3,2,1,0:T(8,128)S(1)} collective-permute-done((f32[3,2,32,128]{3,2,1,0:T(8,128)S(1)}, f32[3,2,32,128]{3,2,1,0:T(8,128)S(1)}, u32[]{:S(2)}, u32[]{:S(2)}) %collective-permute-start.25) | collective-permute-done | bytes 98336 | tf_op jit(solution)/shard_map/ppermute | solution.py:41
  134.1 3.3 %collective-permute-done.26 = bf16[3,2,32,128]{3,2,1,0:T(8,128)(2,1)S(1)} collective-permute-done((bf16[3,2,32,128]{3,2,1,0:T(8,128)(2,1)S(1)}, bf16[3,2,32,128]{3,2,1,0:T(8,128)(2,1)S(1)}, u32[]{:S(2)}, u32[]{:S(2)}) %collective-permute-start.26) | collective-permute-done | bytes 49184 | tf_op jit(solution)/shard_map/ppermute | solution.py:41
  145.1 3.0 %collective-permute-start.30 = (bf16[768,128]{1,0:T(8,128)(2,1)S(1)}, bf16[768,128]{1,0:T(8,128)(2,1)S(1)}, u32[]{:S(2)}, u32[]{:S(2)}) collective-permute-start(bf16[768,128]{1,0:T(8,128)(2,1)S(1)} %pad_maximum_fusion.2.x0), channel_id=1, source_target_pairs={{0,3},{1,2},{2,1},{3,0},{4,7},{5,6},{6,5},{7,4},{8,11},{9,10},{10,... | collective-permute-start | bytes 589832 | tf_op jit(solution)/shard_map/ppermute | solution.py:41
  148.0 2.9 %collective-permute-done.32.x3 = bf16[768,128]{1,0:T(8,128)(2,1)S(1)} collective-permute-done((bf16[768,128]{1,0:T(8,128)(2,1)S(1)}, bf16[768,128]{1,0:T(8,128)(2,1)S(1)}, u32[]{:S(2)}, u32[]{:S(2)}) %collective-permute-start.32) | collective-permute-done | bytes 196640 | tf_op jit(solution)/shard_map/ppermute | solution.py:41
  152.9 3.4 %product.6 = (f32[3,2,32,128]{3,2,1,0:T(8,128)S(1)}, f32[3,2,32,128]{3,2,1,0:T(8,128)S(1)}, f32[3,2,32,128]{3,2,1,0:T(8,128)S(1)}, f32[3,2,32,128]{3,2,1,0:T(8,128)S(1)}) custom-call(s32[1]{0:T(128)} %bitcast.own_ref, bf16[768,128]{1,0:T(8,128)(2,1)S(1)} %pad_maximum_fusion.2.x0, bf16[768,128]{1,0:T(8,128)(2,1)S(1)} %collective-permute-done.30.x1, ...), custom_call_target="tpu_custom_call" | custom-call | tf_op jit(solution)/shard_map/product/pallas_call | solution.py:158
  156.7 2.3 %collective-permute-start.35 = (f32[3,2,32,128]{3,2,1,0:T(8,128)S(1)}, f32[3,2,32,128]{3,2,1,0:T(8,128)S(1)}, u32[]{:S(2)}, u32[]{:S(2)}) collective-permute-start(f32[3,2,32,128]{3,2,1,0:T(8,128)S(1)} %get-tuple-element.40), channel_id=1, source_target_pairs={{0,5},{1,4},{2,7},{3,6},{4,1},{5,0},{6,3},{7,2},{8,13},{9,12},{10,... | collective-permute-start | bytes 294920 | tf_op jit(solution)/shard_map/ppermute | solution.py:41
  170.8 3.3 %collective-permute-done.41.x3 = bf16[768,128]{1,0:T(8,128)(2,1)S(1)} collective-permute-done((bf16[768,128]{1,0:T(8,128)(2,1)S(1)}, bf16[768,128]{1,0:T(8,128)(2,1)S(1)}, u32[]{:S(2)}, u32[]{:S(2)}) %collective-permute-start.41) | collective-permute-done | bytes 196640 | tf_op jit(solution)/shard_map/ppermute | solution.py:41
  176.1 4.0 %product.7 = (f32[3,2,32,128]{3,2,1,0:T(8,128)S(1)}, f32[3,2,32,128]{3,2,1,0:T(8,128)}, f32[3,2,32,128]{3,2,1,0:T(8,128)S(1)}, f32[3,2,32,128]{3,2,1,0:T(8,128)S(1)}) custom-call(s32[1]{0:T(128)} %bitcast.9.own_ref, bf16[768,128]{1,0:T(8,128)(2,1)S(1)} %pad_maximum_fusion.3.x0, bf16[768,128]{1,0:T(8,128)(2,1)S(1)} %collective-permute-done.39.x1, ...), custom_call_target="tpu_custom_call" | custom-call | tf_op jit(solution)/shard_map/product/pallas_call | solution.py:158
  181.6 3.6 %collective-permute-start.44 = (f32[3,2,32,128]{3,2,1,0:T(8,128)S(1)}, f32[3,2,32,128]{3,2,1,0:T(8,128)S(1)}, u32[]{:S(2)}, u32[]{:S(2)}) collective-permute-start(f32[3,2,32,128]{3,2,1,0:T(8,128)S(1)} %get-tuple-element.44), channel_id=1, source_target_pairs={{0,15},{1,14},{2,13},{3,12},{4,11},{5,10},{6,9},{7,8},{8,7},{9,6},... | collective-permute-start | bytes 294920 | tf_op jit(solution)/shard_map/ppermute | solution.py:41
  189.3 15.7 %collective-permute-start.45 = (bf16[3,2,32,128]{3,2,1,0:T(8,128)(2,1)S(1)}, bf16[3,2,32,128]{3,2,1,0:T(8,128)(2,1)S(1)}, u32[]{:S(2)}, u32[]{:S(2)}) collective-permute-start(bf16[3,2,32,128]{3,2,1,0:T(8,128)(2,1)S(1)} %get-tuple-element.45), channel_id=1, source_target_pairs={{0,64},{1,65},{2,66},{3,67},{4,68},{5,69},{6,70},{7,71},{8,72},{9,... | collective-permute-start | bytes 147464 | tf_op jit(solution)/shard_map/ppermute | solution.py:41
  (111 shorter events, 59.8 us)
Async XLA Ops:
  13.7 15.9 %collective-permute-start.6 = (bf16[2048,256]{1,0:T(8,128)(2,1)}, bf16[2048,256]{1,0:T(8,128)(2,1)S(1)}, u32[]{:S(2)}, u32[]{:S(2)}) collective-permute-start(bf16[2048,256]{1,0:T(8,128)(2,1)} %get-tuple-element.26), channel_id=1, source_target_pairs={{0,1},{1,0},{2,3},{3,2},{4,5},{5,4},{6,7},{7,6},{8,9},{9,8},{10,11... | collective-permute-start | bytes 3145736 | tf_op jit(solution)/shard_map/ppermute | solution.py:41
  17.3 15.1 %collective-permute-start.7 = (bf16[2048,256]{1,0:T(8,128)(2,1)}, bf16[2048,256]{1,0:T(8,128)(2,1)S(1)}, u32[]{:S(2)}, u32[]{:S(2)}) collective-permute-start(bf16[2048,256]{1,0:T(8,128)(2,1)} %get-tuple-element.27), channel_id=1, source_target_pairs={{0,4},{1,5},{2,6},{3,7},{4,0},{5,1},{6,2},{7,3},{8,12},{9,13},{10,... | collective-permute-start | bytes 3145736 | tf_op jit(solution)/shard_map/ppermute | solution.py:41
  19.7 23.5 %collective-permute-start.8 = (bf16[2048,256]{1,0:T(8,128)(2,1)}, bf16[2048,256]{1,0:T(8,128)(2,1)S(1)}, u32[]{:S(2)}, u32[]{:S(2)}) collective-permute-start(bf16[2048,256]{1,0:T(8,128)(2,1)} %get-tuple-element.28), channel_id=1, source_target_pairs={{0,5},{1,4},{2,7},{3,6},{4,1},{5,0},{6,3},{7,2},{8,13},{9,12},{10,... | collective-permute-start | bytes 3145736 | tf_op jit(solution)/shard_map/ppermute | solution.py:41
  19.7 59.1 %collective-permute-start.9 = (bf16[2048,256]{1,0:T(8,128)(2,1)}, bf16[2048,256]{1,0:T(8,128)(2,1)}, u32[]{:S(2)}, u32[]{:S(2)}) collective-permute-start(bf16[2048,256]{1,0:T(8,128)(2,1)} %get-tuple-element.25.refs_0_), channel_id=1, source_target_pairs={{0,64},{1,65},{2,66},{3,67},{4,68},{5,69},{6,70},{7,71},{8,72},{9,... | collective-permute-start | bytes 3145736 | tf_op jit(solution)/shard_map/ppermute | solution.py:41
  29.6 49.2 %collective-permute-start.10 = (bf16[2048,256]{1,0:T(8,128)(2,1)S(1)}, bf16[2048,256]{1,0:T(8,128)(2,1)}, u32[]{:S(2)}, u32[]{:S(2)}) collective-permute-start(bf16[2048,256]{1,0:T(8,128)(2,1)S(1)} %collective-permute-done.6.refs_1_), channel_id=1, source_target_pairs={{0,64},{1,65},{2,66},{3,67},{4,68},{5,69},{6,70},{7,71},{8,72},{9,... | collective-permute-start | bytes 3145736 | tf_op jit(solution)/shard_map/ppermute | solution.py:41
  32.3 46.5 %collective-permute-start.11 = (bf16[2048,256]{1,0:T(8,128)(2,1)S(1)}, bf16[2048,256]{1,0:T(8,128)(2,1)}, u32[]{:S(2)}, u32[]{:S(2)}) collective-permute-start(bf16[2048,256]{1,0:T(8,128)(2,1)S(1)} %collective-permute-done.7.refs_2_), channel_id=1, source_target_pairs={{0,64},{1,65},{2,66},{3,67},{4,68},{5,69},{6,70},{7,71},{8,72},{9,... | collective-permute-start | bytes 3145736 | tf_op jit(solution)/shard_map/ppermute | solution.py:41
  43.3 35.6 %collective-permute-start.12 = (bf16[2048,256]{1,0:T(8,128)(2,1)S(1)}, bf16[2048,256]{1,0:T(8,128)(2,1)}, u32[]{:S(2)}, u32[]{:S(2)}) collective-permute-start(bf16[2048,256]{1,0:T(8,128)(2,1)S(1)} %collective-permute-done.8.refs_3_), channel_id=1, source_target_pairs={{0,64},{1,65},{2,66},{3,67},{4,68},{5,69},{6,70},{7,71},{8,72},{9,... | collective-permute-start | bytes 3145736 | tf_op jit(solution)/shard_map/ppermute | solution.py:41
  45.6 5.1 %collective-permute-start.2 = (bf16[192,128]{1,0:T(8,128)(2,1)S(1)}, bf16[192,128]{1,0:T(8,128)(2,1)S(1)}, u32[]{:S(2)}, u32[]{:S(2)}) collective-permute-start(bf16[192,128]{1,0:T(8,128)(2,1)S(1)} %bitcast.36), channel_id=1, source_target_pairs={{0,48},{1,49},{2,50},{3,51},{4,52},{5,53},{6,54},{7,55},{8,56},{9,... | collective-permute-start | bytes 147464 | tf_op jit(solution)/shard_map/ppermute | solution.py:41
  58.0 7.9 %collective-permute-start.5 = (bf16[768,128]{1,0:T(8,128)(2,1)S(1)}, bf16[768,128]{1,0:T(8,128)(2,1)S(1)}, u32[]{:S(2)}, u32[]{:S(2)}) collective-permute-start(bf16[768,128]{1,0:T(8,128)(2,1)S(1)} %pad_maximum_fusion.x0), channel_id=1, source_target_pairs={{0,15},{1,14},{2,13},{3,12},{4,11},{5,10},{6,9},{7,8},{8,7},{9,6},... | collective-permute-start | bytes 589832 | tf_op jit(solution)/shard_map/ppermute | solution.py:41
  66.6 5.7 %collective-permute-start.4 = (bf16[768,128]{1,0:T(8,128)(2,1)S(1)}, bf16[768,128]{1,0:T(8,128)(2,1)S(1)}, u32[]{:S(2)}, u32[]{:S(2)}) collective-permute-start(bf16[768,128]{1,0:T(8,128)(2,1)S(1)} %pad_maximum_fusion.x0), channel_id=1, source_target_pairs={{0,12},{1,13},{2,14},{3,15},{4,8},{5,9},{6,10},{7,11},{8,4},{9,5},... | collective-permute-start | bytes 589832 | tf_op jit(solution)/shard_map/ppermute | solution.py:41
  73.0 5.8 %collective-permute-start.3 = (bf16[768,128]{1,0:T(8,128)(2,1)S(1)}, bf16[768,128]{1,0:T(8,128)(2,1)}, u32[]{:S(2)}, u32[]{:S(2)}) collective-permute-start(bf16[768,128]{1,0:T(8,128)(2,1)S(1)} %pad_maximum_fusion.x0), channel_id=1, source_target_pairs={{0,3},{1,2},{2,1},{3,0},{4,7},{5,6},{6,5},{7,4},{8,11},{9,10},{10,... | collective-permute-start | bytes 589832 | tf_op jit(solution)/shard_map/ppermute | solution.py:41
  86.7 10.6 %collective-permute-start.13 = (f32[3,2,32,128]{3,2,1,0:T(8,128)S(1)}, f32[3,2,32,128]{3,2,1,0:T(8,128)S(1)}, u32[]{:S(2)}, u32[]{:S(2)}) collective-permute-start(f32[3,2,32,128]{3,2,1,0:T(8,128)S(1)} %get-tuple-element.30), channel_id=1, source_target_pairs={{0,1},{1,0},{2,3},{3,2},{4,5},{5,4},{6,7},{7,6},{8,9},{9,8},{10,11... | collective-permute-start | bytes 294920 | tf_op jit(solution)/shard_map/ppermute | solution.py:41
  86.8 10.5 %collective-permute-start.14 = (f32[3,2,32,128]{3,2,1,0:T(8,128)S(1)}, f32[3,2,32,128]{3,2,1,0:T(8,128)S(1)}, u32[]{:S(2)}, u32[]{:S(2)}) collective-permute-start(f32[3,2,32,128]{3,2,1,0:T(8,128)S(1)} %get-tuple-element.31), channel_id=1, source_target_pairs={{0,4},{1,5},{2,6},{3,7},{4,0},{5,1},{6,2},{7,3},{8,12},{9,13},{10,... | collective-permute-start | bytes 294920 | tf_op jit(solution)/shard_map/ppermute | solution.py:41
  86.9 10.4 %collective-permute-start.15 = (f32[3,2,32,128]{3,2,1,0:T(8,128)S(1)}, f32[3,2,32,128]{3,2,1,0:T(8,128)S(1)}, u32[]{:S(2)}, u32[]{:S(2)}) collective-permute-start(f32[3,2,32,128]{3,2,1,0:T(8,128)S(1)} %get-tuple-element.32), channel_id=1, source_target_pairs={{0,5},{1,4},{2,7},{3,6},{4,1},{5,0},{6,3},{7,2},{8,13},{9,12},{10,... | collective-permute-start | bytes 294920 | tf_op jit(solution)/shard_map/ppermute | solution.py:41
  89.5 7.8 %collective-permute-start.16 = (bf16[3,2,32,128]{3,2,1,0:T(8,128)(2,1)S(1)}, bf16[3,2,32,128]{3,2,1,0:T(8,128)(2,1)S(1)}, u32[]{:S(2)}, u32[]{:S(2)}) collective-permute-start(bf16[3,2,32,128]{3,2,1,0:T(8,128)(2,1)S(1)} %dynamic-slice_bitcast_fusion), channel_id=1, source_target_pairs={{0,64},{1,65},{2,66},{3,67},{4,68},{5,69},{6,70},{7,71},{8,72},{9,... | collective-permute-start | bytes 147464 | tf_op jit(solution)/shard_map/ppermute | solution.py:41
  97.4 5.2 %collective-permute-start.19 = (bf16[192,128]{1,0:T(8,128)(2,1)S(1)}, bf16[192,128]{1,0:T(8,128)(2,1)S(1)}, u32[]{:S(2)}, u32[]{:S(2)}) collective-permute-start(bf16[192,128]{1,0:T(8,128)(2,1)S(1)} %bitcast.28), channel_id=1, source_target_pairs={{0,48},{1,49},{2,50},{3,51},{4,52},{5,53},{6,54},{7,55},{8,56},{9,... | collective-permute-start | bytes 147464 | tf_op jit(solution)/shard_map/ppermute | solution.py:41
  105.4 5.7 %collective-permute-start.22 = (bf16[768,128]{1,0:T(8,128)(2,1)S(1)}, bf16[768,128]{1,0:T(8,128)(2,1)}, u32[]{:S(2)}, u32[]{:S(2)}) collective-permute-start(bf16[768,128]{1,0:T(8,128)(2,1)S(1)} %pad_maximum_fusion.1.x0), channel_id=1, source_target_pairs={{0,5},{1,4},{2,7},{3,6},{4,1},{5,0},{6,3},{7,2},{8,13},{9,12},{10,... | collective-permute-start | bytes 589832 | tf_op jit(solution)/shard_map/ppermute | solution.py:41
  105.5 6.6 %collective-permute-start.21 = (bf16[768,128]{1,0:T(8,128)(2,1)S(1)}, bf16[768,128]{1,0:T(8,128)(2,1)}, u32[]{:S(2)}, u32[]{:S(2)}) collective-permute-start(bf16[768,128]{1,0:T(8,128)(2,1)S(1)} %pad_maximum_fusion.1.x0), channel_id=1, source_target_pairs={{0,4},{1,5},{2,6},{3,7},{4,0},{5,1},{6,2},{7,3},{8,12},{9,13},{10,... | collective-permute-start | bytes 589832 | tf_op jit(solution)/shard_map/ppermute | solution.py:41
  106.8 6.7 %collective-permute-start.20 = (bf16[768,128]{1,0:T(8,128)(2,1)S(1)}, bf16[768,128]{1,0:T(8,128)(2,1)}, u32[]{:S(2)}, u32[]{:S(2)}) collective-permute-start(bf16[768,128]{1,0:T(8,128)(2,1)S(1)} %pad_maximum_fusion.1.x0), channel_id=1, source_target_pairs={{0,1},{1,0},{2,3},{3,2},{4,5},{5,4},{6,7},{7,6},{8,9},{9,8},{10,11... | collective-permute-start | bytes 589832 | tf_op jit(solution)/shard_map/ppermute | solution.py:41
  118.4 6.3 %collective-permute-start.23 = (f32[3,2,32,128]{3,2,1,0:T(8,128)S(1)}, f32[3,2,32,128]{3,2,1,0:T(8,128)S(1)}, u32[]{:S(2)}, u32[]{:S(2)}) collective-permute-start(f32[3,2,32,128]{3,2,1,0:T(8,128)S(1)} %get-tuple-element.34), channel_id=1, source_target_pairs={{0,3},{1,2},{2,1},{3,0},{4,7},{5,6},{6,5},{7,4},{8,11},{9,10},{10,... | collective-permute-start | bytes 294920 | tf_op jit(solution)/shard_map/ppermute | solution.py:41
  124.7 7.3 %collective-permute-start.25 = (f32[3,2,32,128]{3,2,1,0:T(8,128)S(1)}, f32[3,2,32,128]{3,2,1,0:T(8,128)S(1)}, u32[]{:S(2)}, u32[]{:S(2)}) collective-permute-start(f32[3,2,32,128]{3,2,1,0:T(8,128)S(1)} %get-tuple-element.36), channel_id=1, source_target_pairs={{0,15},{1,14},{2,13},{3,12},{4,11},{5,10},{6,9},{7,8},{8,7},{9,6},... | collective-permute-start | bytes 294920 | tf_op jit(solution)/shard_map/ppermute | solution.py:41
  132.1 5.2 %collective-permute-start.26 = (bf16[3,2,32,128]{3,2,1,0:T(8,128)(2,1)S(1)}, bf16[3,2,32,128]{3,2,1,0:T(8,128)(2,1)S(1)}, u32[]{:S(2)}, u32[]{:S(2)}) collective-permute-start(bf16[3,2,32,128]{3,2,1,0:T(8,128)(2,1)S(1)} %fusion.2), channel_id=1, source_target_pairs={{0,160},{1,161},{2,162},{3,163},{4,164},{5,165},{6,166},{7,167},{8... | collective-permute-start | bytes 147464 | tf_op jit(solution)/shard_map/ppermute | solution.py:41
  142.9 8.0 %collective-permute-start.32 = (bf16[768,128]{1,0:T(8,128)(2,1)S(1)}, bf16[768,128]{1,0:T(8,128)(2,1)S(1)}, u32[]{:S(2)}, u32[]{:S(2)}) collective-permute-start(bf16[768,128]{1,0:T(8,128)(2,1)S(1)} %pad_maximum_fusion.2.x0), channel_id=1, source_target_pairs={{0,15},{1,14},{2,13},{3,12},{4,11},{5,10},{6,9},{7,8},{8,7},{9,6},... | collective-permute-start | bytes 589832 | tf_op jit(solution)/shard_map/ppermute | solution.py:41
  143.4 7.5 %collective-permute-start.31 = (bf16[768,128]{1,0:T(8,128)(2,1)S(1)}, bf16[768,128]{1,0:T(8,128)(2,1)S(1)}, u32[]{:S(2)}, u32[]{:S(2)}) collective-permute-start(bf16[768,128]{1,0:T(8,128)(2,1)S(1)} %pad_maximum_fusion.2.x0), channel_id=1, source_target_pairs={{0,12},{1,13},{2,14},{3,15},{4,8},{5,9},{6,10},{7,11},{8,4},{9,5},... | collective-permute-start | bytes 589832 | tf_op jit(solution)/shard_map/ppermute | solution.py:41
  145.1 7.9 %collective-permute-start.30 = (bf16[768,128]{1,0:T(8,128)(2,1)S(1)}, bf16[768,128]{1,0:T(8,128)(2,1)S(1)}, u32[]{:S(2)}, u32[]{:S(2)}) collective-permute-start(bf16[768,128]{1,0:T(8,128)(2,1)S(1)} %pad_maximum_fusion.2.x0), channel_id=1, source_target_pairs={{0,3},{1,2},{2,1},{3,0},{4,7},{5,6},{6,5},{7,4},{8,11},{9,10},{10,... | collective-permute-start | bytes 589832 | tf_op jit(solution)/shard_map/ppermute | solution.py:41
  156.7 5.4 %collective-permute-start.35 = (f32[3,2,32,128]{3,2,1,0:T(8,128)S(1)}, f32[3,2,32,128]{3,2,1,0:T(8,128)S(1)}, u32[]{:S(2)}, u32[]{:S(2)}) collective-permute-start(f32[3,2,32,128]{3,2,1,0:T(8,128)S(1)} %get-tuple-element.40), channel_id=1, source_target_pairs={{0,5},{1,4},{2,7},{3,6},{4,1},{5,0},{6,3},{7,2},{8,13},{9,12},{10,... | collective-permute-start | bytes 294920 | tf_op jit(solution)/shard_map/ppermute | solution.py:41
  168.1 6.0 %collective-permute-start.41 = (bf16[768,128]{1,0:T(8,128)(2,1)S(1)}, bf16[768,128]{1,0:T(8,128)(2,1)S(1)}, u32[]{:S(2)}, u32[]{:S(2)}) collective-permute-start(bf16[768,128]{1,0:T(8,128)(2,1)S(1)} %pad_maximum_fusion.3.x0), channel_id=1, source_target_pairs={{0,5},{1,4},{2,7},{3,6},{4,1},{5,0},{6,3},{7,2},{8,13},{9,12},{10,... | collective-permute-start | bytes 589832 | tf_op jit(solution)/shard_map/ppermute | solution.py:41
  169.5 5.6 %collective-permute-start.40 = (bf16[768,128]{1,0:T(8,128)(2,1)S(1)}, bf16[768,128]{1,0:T(8,128)(2,1)S(1)}, u32[]{:S(2)}, u32[]{:S(2)}) collective-permute-start(bf16[768,128]{1,0:T(8,128)(2,1)S(1)} %pad_maximum_fusion.3.x0), channel_id=1, source_target_pairs={{0,4},{1,5},{2,6},{3,7},{4,0},{5,1},{6,2},{7,3},{8,12},{9,13},{10,... | collective-permute-start | bytes 589832 | tf_op jit(solution)/shard_map/ppermute | solution.py:41
  169.7 6.5 %collective-permute-start.39 = (bf16[768,128]{1,0:T(8,128)(2,1)S(1)}, bf16[768,128]{1,0:T(8,128)(2,1)S(1)}, u32[]{:S(2)}, u32[]{:S(2)}) collective-permute-start(bf16[768,128]{1,0:T(8,128)(2,1)S(1)} %pad_maximum_fusion.3.x0), channel_id=1, source_target_pairs={{0,1},{1,0},{2,3},{3,2},{4,5},{5,4},{6,7},{7,6},{8,9},{9,8},{10,11... | collective-permute-start | bytes 589832 | tf_op jit(solution)/shard_map/ppermute | solution.py:41
  180.1 5.1 %collective-permute-start.42 = (f32[3,2,32,128]{3,2,1,0:T(8,128)}, f32[3,2,32,128]{3,2,1,0:T(8,128)S(1)}, u32[]{:S(2)}, u32[]{:S(2)}) collective-permute-start(f32[3,2,32,128]{3,2,1,0:T(8,128)} %get-tuple-element.42), channel_id=1, source_target_pairs={{0,3},{1,2},{2,1},{3,0},{4,7},{5,6},{6,5},{7,4},{8,11},{9,10},{10,... | collective-permute-start | bytes 294920 | tf_op jit(solution)/shard_map/ppermute | solution.py:41
  181.6 6.8 %collective-permute-start.44 = (f32[3,2,32,128]{3,2,1,0:T(8,128)S(1)}, f32[3,2,32,128]{3,2,1,0:T(8,128)S(1)}, u32[]{:S(2)}, u32[]{:S(2)}) collective-permute-start(f32[3,2,32,128]{3,2,1,0:T(8,128)S(1)} %get-tuple-element.44), channel_id=1, source_target_pairs={{0,15},{1,14},{2,13},{3,12},{4,11},{5,10},{6,9},{7,8},{8,7},{9,6},... | collective-permute-start | bytes 294920 | tf_op jit(solution)/shard_map/ppermute | solution.py:41
  189.3 16.6 %collective-permute-start.45 = (bf16[3,2,32,128]{3,2,1,0:T(8,128)(2,1)S(1)}, bf16[3,2,32,128]{3,2,1,0:T(8,128)(2,1)S(1)}, u32[]{:S(2)}, u32[]{:S(2)}) collective-permute-start(bf16[3,2,32,128]{3,2,1,0:T(8,128)(2,1)S(1)} %get-tuple-element.45), channel_id=1, source_target_pairs={{0,64},{1,65},{2,66},{3,67},{4,68},{5,69},{6,70},{7,71},{8,72},{9,... | collective-permute-start | bytes 147464 | tf_op jit(solution)/shard_map/ppermute | solution.py:41
  (30 other events, 262.7 us)
where the time goes:
time: 207 us
  waiting for transfers between devices  85 us (41%)
  starting transfers between devices  83.5 us (40%)
  Pallas kernels  26.7 us (13%)
  local copies, waits for them, and re-layouts  7.88 us (4%)
  other arithmetic  3.33 us (2%)
    ppermute x46, waiting for transfers between devices, exchange(): return lax.ppermute(value, AXES, pairs)  85 us
    ppermute x46, starting transfers between devices, exchange(): return lax.ppermute(value, AXES, pairs)  83.5 us
    pallas_call x4, Pallas kernels, product(): pl.pallas_call(product_kernel, out_shape=[jax.ShapeDtypeStruct((3, 2, wid...  14.5 us
    pallas_call x1, Pallas kernels, reorder(): pl.pallas_call(reorder_kernel, out_shape=[jax.ShapeDtypeStruct((columns /...  12.1 us
    unnamed x32, local copies, waits for them, and re-layouts  7.87 us
  transfers between devices with their start and end apart: 46, of which 33 were waited for; matrix products, arithmetic and copies ran while one was open for 0% of the time, Pallas kernels for 0%

commit v1 on v0

--- a/solution.py
+++ b/solution.py
@@ -1,3 +1,5 @@
+import functools
+
 import jax
 import jax.numpy as jnp
 from jax import lax
@@ -124,18 +126,19 @@
         cost_estimate=pl.CostEstimate(
             flops=0, bytes_accessed=40 * 1024 * 1024, transcendentals=0
         ),
+        compiler_params=pltpu.CompilerParams(vmem_limit_bytes=24 * 1024 * 1024),
         name="reorder",
     )(slots, matrix)
 
 
-def product_kernel(own_ref, x0, x1, x2, x3, *refs):
+def product_kernel(outer, own_ref, x0, x1, x2, x3, *refs):
     own, other, outs, joined = refs[:4], refs[4:8], refs[8:12], refs[12]
     use_own = own_ref[0] == 1
     width = joined.shape[0]
     for at, piece in enumerate((x0, x1, x2, x3)):
-        for z in range(4):
-            start = (z * 4 + at) * LANES
-            joined[:, start : start + LANES] = piece[z * width : (z + 1) * width]
+        for n in range(4):
+            start = (at * outer + n * (4 // outer)) * LANES
+            joined[:, start : start + LANES] = piece[n * width : (n + 1) * width]
     half = width // 6
 
     for weights, wanted in ((own, use_own), (other, jnp.logical_not(use_own))):
@@ -151,17 +154,17 @@
                 outs[m][:, 1] = both[:, 1, :, :LANES] + both[:, 0, :, LANES:]
 
 
-def product(use_own, pieces, own, other):
+def product(step, use_own, pieces, own, other):
     depth = own[0].shape[0]
     width = pieces[0].shape[0] // 4
     vmem = pl.BlockSpec(memory_space=pltpu.VMEM)
     return pl.pallas_call(
-        product_kernel,
+        functools.partial(product_kernel, 4 if step == 0 else 1),
         out_shape=[jax.ShapeDtypeStruct((3, 2, width // 6, LANES), jnp.float32)] * 4,
         in_specs=[pl.BlockSpec(memory_space=pltpu.SMEM)] + [vmem] * 12,
         out_specs=[vmem] * 4,
         scratch_shapes=[pltpu.VMEM((width, depth), jnp.bfloat16)],
-        compiler_params=pltpu.CompilerParams(vmem_limit_bytes=24 * 1024 * 1024),
+        compiler_params=pltpu.CompilerParams(vmem_limit_bytes=12 * 1024 * 1024),
         name="product",
     )(use_own, *pieces, *own, *other)
 
@@ -169,9 +172,10 @@
 def gather(step, value):
     parity = step & 1
     flat = value.reshape(-1, LANES)
-    parts = [flat] + [exchange(flat, to_group(parity, z << 2)) for z in (1, 2, 3)]
+    inner, outer = (1, 4) if step == 0 else (4, 1)
+    parts = [flat] + [exchange(flat, to_group(parity, n * inner)) for n in (1, 2, 3)]
     joined = jnp.concatenate(parts, axis=0)
-    return [joined] + [exchange(joined, to_group(parity, at)) for at in (1, 2, 3)]
+    return [joined] + [exchange(joined, to_group(parity, n * outer)) for n in (1, 2, 3)]
 
 
 def sweep(rhs, operator, sources, skeleton):
@@ -209,7 +213,7 @@
             value = exchange(value, other_half)
         if step:
             pieces = gather(step, value)
-        partial = product(use_own, pieces, own, other)
+        partial = product(step, use_own, pieces, own, other)
         total = partial[0]
         for m in (1, 2, 3):
             total = total + exchange(partial[m], to_member(parity, m))

time: 207 us -> 207 us (level)
  starting transfers between devices: 83.5 us -> 87.1 us
  local copies, waits for them, and re-layouts: 7.88 us -> 5.42 us
  waiting for transfers between devices: 85 us -> 87.1 us
    ppermute x46, starting transfers between devices: 83.5 us -> 87.1 us  [exchange(): return lax.ppermute(value, AXES, pairs)]
    pallas_call x1, Pallas kernels: 12.1 us -> 8.95 us  [reorder(): pl.pallas_call(reorder_kernel, out_shape=[jax.ShapeDtypeStruct((columns /...]
    unnamed x32 -> x24, local copies, waits for them, and re-layouts: 7.87 us -> 5.41 us
    ppermute x46, waiting for transfers between devices: 85 us -> 87.1 us  [exchange(): return lax.ppermute(value, AXES, pairs)]
where the time goes in v1:
time: 207 us
  starting transfers between devices  87.1 us (42%)
  waiting for transfers between devices  87.1 us (42%)
  Pallas kernels  24.7 us (12%)
  local copies, waits for them, and re-layouts  5.42 us (3%)
  other arithmetic  2.71 us (1%)
    ppermute x46, waiting for transfers between devices, exchange(): return lax.ppermute(value, AXES, pairs)  87.1 us
    ppermute x46, starting transfers between devices, exchange(): return lax.ppermute(value, AXES, pairs)  87.1 us
    pallas_call x4, Pallas kernels, product(): pl.pallas_call(functools.partial(product_kernel, 4 if step == 0 else 1),...  15.8 us
    pallas_call x1, Pallas kernels, reorder(): pl.pallas_call(reorder_kernel, out_shape=[jax.ShapeDtypeStruct((columns /...  8.95 us
    unnamed x24, local copies, waits for them, and re-layouts  5.41 us
  transfers between devices with their start and end apart: 46, of which 33 were waited for; matrix products, arithmetic and copies ran while one was open for 0% of the time, Pallas kernels for 0%

profile of v1, /device:TPU:1, one launch (start us, length us, event | category | flops | bytes accessed | tf_op | source)
XLA Modules:
  0.0 207.3 jit_solution(9920446367477366975)
XLA Ops:
  3.1 8.9 %reorder.1 = (bf16[2048,256]{1,0:T(8,128)(2,1)S(1)}, bf16[2048,256]{1,0:T(8,128)(2,1)S(1)}, bf16[2048,256]{1,0:T(8,128)(2,1)S(1)}, bf16[2048,256]{1,0:T(8,128)(2,1)S(1)}) custom-call(s32[8192]{0:T(1024)S(1)} %fusion.10.slot_ref, bf16[2,128,8192]{2,1,0:T(8,128)(2,1)S(1)} %bitcast.27), custom_call_target="tpu_custom_call" | custom-call | bytes 41943040 | tf_op jit(solution)/shard_map/reorder/pallas_call | solution.py:116
  12.1 3.6 %collective-permute-start.6 = (bf16[2048,256]{1,0:T(8,128)(2,1)S(1)}, bf16[2048,256]{1,0:T(8,128)(2,1)S(1)}, u32[]{:S(2)}, u32[]{:S(2)}) collective-permute-start(bf16[2048,256]{1,0:T(8,128)(2,1)S(1)} %get-tuple-element.26), channel_id=1, source_target_pairs={{0,1},{1,0},{2,3},{3,2},{4,5},{5,4},{6,7},{7,6},{8,9},{9,8},{10,11... | collective-permute-start | bytes 3145736 | tf_op jit(solution)/shard_map/ppermute | solution.py:43
  15.7 2.5 %collective-permute-start.7 = (bf16[2048,256]{1,0:T(8,128)(2,1)S(1)}, bf16[2048,256]{1,0:T(8,128)(2,1)S(1)}, u32[]{:S(2)}, u32[]{:S(2)}) collective-permute-start(bf16[2048,256]{1,0:T(8,128)(2,1)S(1)} %get-tuple-element.27), channel_id=1, source_target_pairs={{0,4},{1,5},{2,6},{3,7},{4,0},{5,1},{6,2},{7,3},{8,12},{9,13},{10,... | collective-permute-start | bytes 3145736 | tf_op jit(solution)/shard_map/ppermute | solution.py:43
  18.9 9.1 %collective-permute-done.6.refs_1_ = bf16[2048,256]{1,0:T(8,128)(2,1)S(1)} collective-permute-done((bf16[2048,256]{1,0:T(8,128)(2,1)S(1)}, bf16[2048,256]{1,0:T(8,128)(2,1)S(1)}, u32[]{:S(2)}, u32[]{:S(2)}) %collective-permute-start.6) | collective-permute-done | bytes 1048608 | tf_op jit(solution)/shard_map/ppermute | solution.py:43
  30.6 11.2 %collective-permute-done.8.refs_3_ = bf16[2048,256]{1,0:T(8,128)(2,1)} collective-permute-done((bf16[2048,256]{1,0:T(8,128)(2,1)S(1)}, bf16[2048,256]{1,0:T(8,128)(2,1)}, u32[]{:S(2)}, u32[]{:S(2)}) %collective-permute-start.8) | collective-permute-done | bytes 1048608 | tf_op jit(solution)/shard_map/ppermute | solution.py:43
  43.0 3.6 %collective-permute-start.2 = (bf16[192,128]{1,0:T(8,128)(2,1)S(1)}, bf16[192,128]{1,0:T(8,128)(2,1)S(1)}, u32[]{:S(2)}, u32[]{:S(2)}) collective-permute-start(bf16[192,128]{1,0:T(8,128)(2,1)S(1)} %bitcast.36), channel_id=1, source_target_pairs={{0,15},{1,14},{2,13},{3,12},{4,11},{5,10},{6,9},{7,8},{8,7},{9,6},... | collective-permute-start | bytes 147464 | tf_op jit(solution)/shard_map/ppermute | solution.py:43
  46.6 2.6 %collective-permute-done.2 = bf16[192,128]{1,0:T(8,128)(2,1)S(1)} collective-permute-done((bf16[192,128]{1,0:T(8,128)(2,1)S(1)}, bf16[192,128]{1,0:T(8,128)(2,1)S(1)}, u32[]{:S(2)}, u32[]{:S(2)}) %collective-permute-start.2) | collective-permute-done | bytes 49184 | tf_op jit(solution)/shard_map/ppermute | solution.py:43
  50.6 2.8 %collective-permute-done.1 = bf16[192,128]{1,0:T(8,128)(2,1)S(1)} collective-permute-done((bf16[192,128]{1,0:T(8,128)(2,1)S(1)}, bf16[192,128]{1,0:T(8,128)(2,1)S(1)}, u32[]{:S(2)}, u32[]{:S(2)}) %collective-permute-start.1) | collective-permute-done | bytes 49184 | tf_op jit(solution)/shard_map/ppermute | solution.py:43
  54.8 2.7 %collective-permute-done = bf16[192,128]{1,0:T(8,128)(2,1)S(1)} collective-permute-done((bf16[192,128]{1,0:T(8,128)(2,1)S(1)}, bf16[192,128]{1,0:T(8,128)(2,1)S(1)}, u32[]{:S(2)}, u32[]{:S(2)}) %collective-permute-start) | collective-permute-done | bytes 49184 | tf_op jit(solution)/shard_map/ppermute | solution.py:43
  57.6 3.3 %collective-permute-start.5 = (bf16[768,128]{1,0:T(8,128)(2,1)S(1)}, bf16[768,128]{1,0:T(8,128)(2,1)S(1)}, u32[]{:S(2)}, u32[]{:S(2)}) collective-permute-start(bf16[768,128]{1,0:T(8,128)(2,1)S(1)} %pad_maximum_fusion.x0), channel_id=1, source_target_pairs={{0,48},{1,49},{2,50},{3,51},{4,52},{5,53},{6,54},{7,55},{8,56},{9,... | collective-permute-start | bytes 589832 | tf_op jit(solution)/shard_map/ppermute | solution.py:43
  60.9 3.2 %collective-permute-done.5.x3 = bf16[768,128]{1,0:T(8,128)(2,1)S(1)} collective-permute-done((bf16[768,128]{1,0:T(8,128)(2,1)S(1)}, bf16[768,128]{1,0:T(8,128)(2,1)S(1)}, u32[]{:S(2)}, u32[]{:S(2)}) %collective-permute-start.5) | collective-permute-done | bytes 196640 | tf_op jit(solution)/shard_map/ppermute | solution.py:43
  64.9 8.2 %collective-permute-done.4.x2 = bf16[768,128]{1,0:T(8,128)(2,1)S(1)} collective-permute-done((bf16[768,128]{1,0:T(8,128)(2,1)S(1)}, bf16[768,128]{1,0:T(8,128)(2,1)S(1)}, u32[]{:S(2)}, u32[]{:S(2)}) %collective-permute-start.4) | collective-permute-done | bytes 196640 | tf_op jit(solution)/shard_map/ppermute | solution.py:43
  73.8 5.7 %collective-permute-done.3.x1 = bf16[768,128]{1,0:T(8,128)(2,1)} collective-permute-done((bf16[768,128]{1,0:T(8,128)(2,1)S(1)}, bf16[768,128]{1,0:T(8,128)(2,1)}, u32[]{:S(2)}, u32[]{:S(2)}) %collective-permute-start.3) | collective-permute-done | bytes 196640 | tf_op jit(solution)/shard_map/ppermute | solution.py:43
  81.4 3.8 %product.4 = (f32[3,2,32,128]{3,2,1,0:T(8,128)S(1)}, f32[3,2,32,128]{3,2,1,0:T(8,128)S(1)}, f32[3,2,32,128]{3,2,1,0:T(8,128)S(1)}, f32[3,2,32,128]{3,2,1,0:T(8,128)S(1)}) custom-call(s32[1]{0:T(128)} %bitcast.own_ref, bf16[768,128]{1,0:T(8,128)(2,1)S(1)} %pad_maximum_fusion.x0, bf16[768,128]{1,0:T(8,128)(2,1)} %collective-permute-done.3.x1, ...), custom_call_target="tpu_custom_call" | custom-call | tf_op jit(solution)/shard_map/product/pallas_call | solution.py:161
  85.3 2.5 %collective-permute-start.15 = (f32[3,2,32,128]{3,2,1,0:T(8,128)S(1)}, f32[3,2,32,128]{3,2,1,0:T(8,128)S(1)}, u32[]{:S(2)}, u32[]{:S(2)}) collective-permute-start(f32[3,2,32,128]{3,2,1,0:T(8,128)S(1)} %get-tuple-element.32), channel_id=1, source_target_pairs={{0,5},{1,4},{2,7},{3,6},{4,1},{5,0},{6,3},{7,2},{8,13},{9,12},{10,... | collective-permute-start | bytes 294920 | tf_op jit(solution)/shard_map/ppermute | solution.py:43
  87.9 7.9 %collective-permute-start.16 = (bf16[3,2,32,128]{3,2,1,0:T(8,128)(2,1)S(1)}, bf16[3,2,32,128]{3,2,1,0:T(8,128)(2,1)S(1)}, u32[]{:S(2)}, u32[]{:S(2)}) collective-permute-start(bf16[3,2,32,128]{3,2,1,0:T(8,128)(2,1)S(1)} %dynamic-slice_bitcast_fusion), channel_id=1, source_target_pairs={{0,64},{1,65},{2,66},{3,67},{4,68},{5,69},{6,70},{7,71},{8,72},{9,... | collective-permute-start | bytes 147464 | tf_op jit(solution)/shard_map/ppermute | solution.py:43
  96.8 3.6 %collective-permute-start.19 = (bf16[192,128]{1,0:T(8,128)(2,1)S(1)}, bf16[192,128]{1,0:T(8,128)(2,1)S(1)}, u32[]{:S(2)}, u32[]{:S(2)}) collective-permute-start(bf16[192,128]{1,0:T(8,128)(2,1)S(1)} %bitcast.28), channel_id=1, source_target_pairs={{0,48},{1,49},{2,50},{3,51},{4,52},{5,53},{6,54},{7,55},{8,56},{9,... | collective-permute-start | bytes 147464 | tf_op jit(solution)/shard_map/ppermute | solution.py:43
  102.0 2.4 %collective-permute-done.18 = bf16[192,128]{1,0:T(8,128)(2,1)S(1)} collective-permute-done((bf16[192,128]{1,0:T(8,128)(2,1)S(1)}, bf16[192,128]{1,0:T(8,128)(2,1)S(1)}, u32[]{:S(2)}, u32[]{:S(2)}) %collective-permute-start.18) | collective-permute-done | bytes 49184 | tf_op jit(solution)/shard_map/ppermute | solution.py:43
  107.2 3.0 %collective-permute-done.22.x3 = bf16[768,128]{1,0:T(8,128)(2,1)} collective-permute-done((bf16[768,128]{1,0:T(8,128)(2,1)S(1)}, bf16[768,128]{1,0:T(8,128)(2,1)}, u32[]{:S(2)}, u32[]{:S(2)}) %collective-permute-start.22) | collective-permute-done | bytes 196640 | tf_op jit(solution)/shard_map/ppermute | solution.py:43
  112.2 4.0 %product.5 = (f32[3,2,32,128]{3,2,1,0:T(8,128)S(1)}, f32[3,2,32,128]{3,2,1,0:T(8,128)S(1)}, f32[3,2,32,128]{3,2,1,0:T(8,128)S(1)}, f32[3,2,32,128]{3,2,1,0:T(8,128)S(1)}) custom-call(s32[1]{0:T(128)} %bitcast.9.own_ref, bf16[768,128]{1,0:T(8,128)(2,1)S(1)} %pad_maximum_fusion.1.x0, bf16[768,128]{1,0:T(8,128)(2,1)} %collective-permute-done.20.x1, ...), custom_call_target="tpu_custom_call" | custom-call | tf_op jit(solution)/shard_map/product/pallas_call | solution.py:161
  116.1 2.7 %collective-permute-start.23 = (f32[3,2,32,128]{3,2,1,0:T(8,128)S(1)}, f32[3,2,32,128]{3,2,1,0:T(8,128)S(1)}, u32[]{:S(2)}, u32[]{:S(2)}) collective-permute-start(f32[3,2,32,128]{3,2,1,0:T(8,128)S(1)} %get-tuple-element.34), channel_id=1, source_target_pairs={{0,3},{1,2},{2,1},{3,0},{4,7},{5,6},{6,5},{7,4},{8,11},{9,10},{10,... | collective-permute-start | bytes 294920 | tf_op jit(solution)/shard_map/ppermute | solution.py:43
  118.8 2.5 %collective-permute-start.24 = (f32[3,2,32,128]{3,2,1,0:T(8,128)S(1)}, f32[3,2,32,128]{3,2,1,0:T(8,128)S(1)}, u32[]{:S(2)}, u32[]{:S(2)}) collective-permute-start(f32[3,2,32,128]{3,2,1,0:T(8,128)S(1)} %get-tuple-element.35), channel_id=1, source_target_pairs={{0,12},{1,13},{2,14},{3,15},{4,8},{5,9},{6,10},{7,11},{8,4},{9,5},... | collective-permute-start | bytes 294920 | tf_op jit(solution)/shard_map/ppermute | solution.py:43
  123.5 4.6 %collective-permute-done.25 = f32[3,2,32,128]{3,2,1,0:T(8,128)S(1)} collective-permute-done((f32[3,2,32,128]{3,2,1,0:T(8,128)S(1)}, f32[3,2,32,128]{3,2,1,0:T(8,128)S(1)}, u32[]{:S(2)}, u32[]{:S(2)}) %collective-permute-start.25) | collective-permute-done | bytes 98336 | tf_op jit(solution)/shard_map/ppermute | solution.py:43
  128.1 3.2 %collective-permute-start.26 = (bf16[3,2,32,128]{3,2,1,0:T(8,128)(2,1)S(1)}, bf16[3,2,32,128]{3,2,1,0:T(8,128)(2,1)S(1)}, u32[]{:S(2)}, u32[]{:S(2)}) collective-permute-start(bf16[3,2,32,128]{3,2,1,0:T(8,128)(2,1)S(1)} %fusion.2), channel_id=1, source_target_pairs={{0,160},{1,161},{2,162},{3,163},{4,164},{5,165},{6,166},{7,167},{8... | collective-permute-start | bytes 147464 | tf_op jit(solution)/shard_map/ppermute | solution.py:43
  141.9 2.6 %collective-permute-start.30 = (bf16[768,128]{1,0:T(8,128)(2,1)S(1)}, bf16[768,128]{1,0:T(8,128)(2,1)S(1)}, u32[]{:S(2)}, u32[]{:S(2)}) collective-permute-start(bf16[768,128]{1,0:T(8,128)(2,1)S(1)} %pad_maximum_fusion.2.x0), channel_id=1, source_target_pairs={{0,3},{1,2},{2,1},{3,0},{4,7},{5,6},{6,5},{7,4},{8,11},{9,10},{10,... | collective-permute-start | bytes 589832 | tf_op jit(solution)/shard_map/ppermute | solution.py:43
  144.5 2.9 %collective-permute-done.32.x3 = bf16[768,128]{1,0:T(8,128)(2,1)S(1)} collective-permute-done((bf16[768,128]{1,0:T(8,128)(2,1)S(1)}, bf16[768,128]{1,0:T(8,128)(2,1)S(1)}, u32[]{:S(2)}, u32[]{:S(2)}) %collective-permute-start.32) | collective-permute-done | bytes 196640 | tf_op jit(solution)/shard_map/ppermute | solution.py:43
  149.4 3.7 %product.6 = (f32[3,2,32,128]{3,2,1,0:T(8,128)S(1)}, f32[3,2,32,128]{3,2,1,0:T(8,128)S(1)}, f32[3,2,32,128]{3,2,1,0:T(8,128)S(1)}, f32[3,2,32,128]{3,2,1,0:T(8,128)S(1)}) custom-call(s32[1]{0:T(128)} %bitcast.own_ref, bf16[768,128]{1,0:T(8,128)(2,1)S(1)} %pad_maximum_fusion.2.x0, bf16[768,128]{1,0:T(8,128)(2,1)S(1)} %collective-permute-done.30.x1, ...), custom_call_target="tpu_custom_call" | custom-call | tf_op jit(solution)/shard_map/product/pallas_call | solution.py:161
  153.5 2.3 %collective-permute-start.35 = (f32[3,2,32,128]{3,2,1,0:T(8,128)S(1)}, f32[3,2,32,128]{3,2,1,0:T(8,128)S(1)}, u32[]{:S(2)}, u32[]{:S(2)}) collective-permute-start(f32[3,2,32,128]{3,2,1,0:T(8,128)S(1)} %get-tuple-element.40), channel_id=1, source_target_pairs={{0,5},{1,4},{2,7},{3,6},{4,1},{5,0},{6,3},{7,2},{8,13},{9,12},{10,... | collective-permute-start | bytes 294920 | tf_op jit(solution)/shard_map/ppermute | solution.py:43
  167.9 4.8 %collective-permute-done.41.x3 = bf16[768,128]{1,0:T(8,128)(2,1)S(1)} collective-permute-done((bf16[768,128]{1,0:T(8,128)(2,1)S(1)}, bf16[768,128]{1,0:T(8,128)(2,1)S(1)}, u32[]{:S(2)}, u32[]{:S(2)}) %collective-permute-start.41) | collective-permute-done | bytes 196640 | tf_op jit(solution)/shard_map/ppermute | solution.py:43
  173.8 4.3 %product.7 = (f32[3,2,32,128]{3,2,1,0:T(8,128)S(1)}, f32[3,2,32,128]{3,2,1,0:T(8,128)}, f32[3,2,32,128]{3,2,1,0:T(8,128)S(1)}, f32[3,2,32,128]{3,2,1,0:T(8,128)S(1)}) custom-call(s32[1]{0:T(128)} %bitcast.9.own_ref, bf16[768,128]{1,0:T(8,128)(2,1)S(1)} %pad_maximum_fusion.3.x0, bf16[768,128]{1,0:T(8,128)(2,1)S(1)} %collective-permute-done.39.x1, ...), custom_call_target="tpu_custom_call" | custom-call | tf_op jit(solution)/shard_map/product/pallas_call | solution.py:161
  179.7 3.5 %collective-permute-start.44 = (f32[3,2,32,128]{3,2,1,0:T(8,128)S(1)}, f32[3,2,32,128]{3,2,1,0:T(8,128)S(1)}, u32[]{:S(2)}, u32[]{:S(2)}) collective-permute-start(f32[3,2,32,128]{3,2,1,0:T(8,128)S(1)} %get-tuple-element.44), channel_id=1, source_target_pairs={{0,15},{1,14},{2,13},{3,12},{4,11},{5,10},{6,9},{7,8},{8,7},{9,6},... | collective-permute-start | bytes 294920 | tf_op jit(solution)/shard_map/ppermute | solution.py:43
  187.4 18.3 %collective-permute-start.45 = (bf16[3,2,32,128]{3,2,1,0:T(8,128)(2,1)S(1)}, bf16[3,2,32,128]{3,2,1,0:T(8,128)(2,1)S(1)}, u32[]{:S(2)}, u32[]{:S(2)}) collective-permute-start(bf16[3,2,32,128]{3,2,1,0:T(8,128)(2,1)S(1)} %get-tuple-element.45), channel_id=1, source_target_pairs={{0,64},{1,65},{2,66},{3,67},{4,68},{5,69},{6,70},{7,71},{8,72},{9,... | collective-permute-start | bytes 147464 | tf_op jit(solution)/shard_map/ppermute | solution.py:43
  (103 shorter events, 57.0 us)
Async XLA Ops:
  12.1 15.8 %collective-permute-start.6 = (bf16[2048,256]{1,0:T(8,128)(2,1)S(1)}, bf16[2048,256]{1,0:T(8,128)(2,1)S(1)}, u32[]{:S(2)}, u32[]{:S(2)}) collective-permute-start(bf16[2048,256]{1,0:T(8,128)(2,1)S(1)} %get-tuple-element.26), channel_id=1, source_target_pairs={{0,1},{1,0},{2,3},{3,2},{4,5},{5,4},{6,7},{7,6},{8,9},{9,8},{10,11... | collective-permute-start | bytes 3145736 | tf_op jit(solution)/shard_map/ppermute | solution.py:43
  15.7 14.9 %collective-permute-start.7 = (bf16[2048,256]{1,0:T(8,128)(2,1)S(1)}, bf16[2048,256]{1,0:T(8,128)(2,1)S(1)}, u32[]{:S(2)}, u32[]{:S(2)}) collective-permute-start(bf16[2048,256]{1,0:T(8,128)(2,1)S(1)} %get-tuple-element.27), channel_id=1, source_target_pairs={{0,4},{1,5},{2,6},{3,7},{4,0},{5,1},{6,2},{7,3},{8,12},{9,13},{10,... | collective-permute-start | bytes 3145736 | tf_op jit(solution)/shard_map/ppermute | solution.py:43
  18.2 23.5 %collective-permute-start.8 = (bf16[2048,256]{1,0:T(8,128)(2,1)S(1)}, bf16[2048,256]{1,0:T(8,128)(2,1)}, u32[]{:S(2)}, u32[]{:S(2)}) collective-permute-start(bf16[2048,256]{1,0:T(8,128)(2,1)S(1)} %get-tuple-element.28), channel_id=1, source_target_pairs={{0,5},{1,4},{2,7},{3,6},{4,1},{5,0},{6,3},{7,2},{8,13},{9,12},{10,... | collective-permute-start | bytes 3145736 | tf_op jit(solution)/shard_map/ppermute | solution.py:43
  18.2 61.3 %collective-permute-start.9 = (bf16[2048,256]{1,0:T(8,128)(2,1)S(1)}, bf16[2048,256]{1,0:T(8,128)(2,1)}, u32[]{:S(2)}, u32[]{:S(2)}) collective-permute-start(bf16[2048,256]{1,0:T(8,128)(2,1)S(1)} %get-tuple-element.25.refs_0_), channel_id=1, source_target_pairs={{0,64},{1,65},{2,66},{3,67},{4,68},{5,69},{6,70},{7,71},{8,72},{9,... | collective-permute-start | bytes 3145736 | tf_op jit(solution)/shard_map/ppermute | solution.py:43
  27.9 51.6 %collective-permute-start.10 = (bf16[2048,256]{1,0:T(8,128)(2,1)S(1)}, bf16[2048,256]{1,0:T(8,128)(2,1)}, u32[]{:S(2)}, u32[]{:S(2)}) collective-permute-start(bf16[2048,256]{1,0:T(8,128)(2,1)S(1)} %collective-permute-done.6.refs_1_), channel_id=1, source_target_pairs={{0,64},{1,65},{2,66},{3,67},{4,68},{5,69},{6,70},{7,71},{8,72},{9,... | collective-permute-start | bytes 3145736 | tf_op jit(solution)/shard_map/ppermute | solution.py:43
  30.6 48.9 %collective-permute-start.11 = (bf16[2048,256]{1,0:T(8,128)(2,1)S(1)}, bf16[2048,256]{1,0:T(8,128)(2,1)}, u32[]{:S(2)}, u32[]{:S(2)}) collective-permute-start(bf16[2048,256]{1,0:T(8,128)(2,1)S(1)} %collective-permute-done.7.refs_2_), channel_id=1, source_target_pairs={{0,64},{1,65},{2,66},{3,67},{4,68},{5,69},{6,70},{7,71},{8,72},{9,... | collective-permute-start | bytes 3145736 | tf_op jit(solution)/shard_map/ppermute | solution.py:43
  41.7 37.7 %collective-permute-start.12 = (bf16[2048,256]{1,0:T(8,128)(2,1)}, bf16[2048,256]{1,0:T(8,128)(2,1)}, u32[]{:S(2)}, u32[]{:S(2)}) collective-permute-start(bf16[2048,256]{1,0:T(8,128)(2,1)} %collective-permute-done.8.refs_3_), channel_id=1, source_target_pairs={{0,64},{1,65},{2,66},{3,67},{4,68},{5,69},{6,70},{7,71},{8,72},{9,... | collective-permute-start | bytes 3145736 | tf_op jit(solution)/shard_map/ppermute | solution.py:43
  43.0 6.3 %collective-permute-start.2 = (bf16[192,128]{1,0:T(8,128)(2,1)S(1)}, bf16[192,128]{1,0:T(8,128)(2,1)S(1)}, u32[]{:S(2)}, u32[]{:S(2)}) collective-permute-start(bf16[192,128]{1,0:T(8,128)(2,1)S(1)} %bitcast.36), channel_id=1, source_target_pairs={{0,15},{1,14},{2,13},{3,12},{4,11},{5,10},{6,9},{7,8},{8,7},{9,6},... | collective-permute-start | bytes 147464 | tf_op jit(solution)/shard_map/ppermute | solution.py:43
  57.6 6.5 %collective-permute-start.5 = (bf16[768,128]{1,0:T(8,128)(2,1)S(1)}, bf16[768,128]{1,0:T(8,128)(2,1)S(1)}, u32[]{:S(2)}, u32[]{:S(2)}) collective-permute-start(bf16[768,128]{1,0:T(8,128)(2,1)S(1)} %pad_maximum_fusion.x0), channel_id=1, source_target_pairs={{0,48},{1,49},{2,50},{3,51},{4,52},{5,53},{6,54},{7,55},{8,56},{9,... | collective-permute-start | bytes 589832 | tf_op jit(solution)/shard_map/ppermute | solution.py:43
  64.8 8.3 %collective-permute-start.4 = (bf16[768,128]{1,0:T(8,128)(2,1)S(1)}, bf16[768,128]{1,0:T(8,128)(2,1)S(1)}, u32[]{:S(2)}, u32[]{:S(2)}) collective-permute-start(bf16[768,128]{1,0:T(8,128)(2,1)S(1)} %pad_maximum_fusion.x0), channel_id=1, source_target_pairs={{0,32},{1,33},{2,34},{3,35},{4,36},{5,37},{6,38},{7,39},{8,40},{9,... | collective-permute-start | bytes 589832 | tf_op jit(solution)/shard_map/ppermute | solution.py:43
  73.8 5.7 %collective-permute-start.3 = (bf16[768,128]{1,0:T(8,128)(2,1)S(1)}, bf16[768,128]{1,0:T(8,128)(2,1)}, u32[]{:S(2)}, u32[]{:S(2)}) collective-permute-start(bf16[768,128]{1,0:T(8,128)(2,1)S(1)} %pad_maximum_fusion.x0), channel_id=1, source_target_pairs={{0,16},{1,17},{2,18},{3,19},{4,20},{5,21},{6,22},{7,23},{8,24},{9,... | collective-permute-start | bytes 589832 | tf_op jit(solution)/shard_map/ppermute | solution.py:43
  85.1 11.6 %collective-permute-start.13 = (f32[3,2,32,128]{3,2,1,0:T(8,128)S(1)}, f32[3,2,32,128]{3,2,1,0:T(8,128)S(1)}, u32[]{:S(2)}, u32[]{:S(2)}) collective-permute-start(f32[3,2,32,128]{3,2,1,0:T(8,128)S(1)} %get-tuple-element.30), channel_id=1, source_target_pairs={{0,1},{1,0},{2,3},{3,2},{4,5},{5,4},{6,7},{7,6},{8,9},{9,8},{10,11... | collective-permute-start | bytes 294920 | tf_op jit(solution)/shard_map/ppermute | solution.py:43
  85.2 11.5 %collective-permute-start.14 = (f32[3,2,32,128]{3,2,1,0:T(8,128)S(1)}, f32[3,2,32,128]{3,2,1,0:T(8,128)S(1)}, u32[]{:S(2)}, u32[]{:S(2)}) collective-permute-start(f32[3,2,32,128]{3,2,1,0:T(8,128)S(1)} %get-tuple-element.31), channel_id=1, source_target_pairs={{0,4},{1,5},{2,6},{3,7},{4,0},{5,1},{6,2},{7,3},{8,12},{9,13},{10,... | collective-permute-start | bytes 294920 | tf_op jit(solution)/shard_map/ppermute | solution.py:43
  85.3 11.4 %collective-permute-start.15 = (f32[3,2,32,128]{3,2,1,0:T(8,128)S(1)}, f32[3,2,32,128]{3,2,1,0:T(8,128)S(1)}, u32[]{:S(2)}, u32[]{:S(2)}) collective-permute-start(f32[3,2,32,128]{3,2,1,0:T(8,128)S(1)} %get-tuple-element.32), channel_id=1, source_target_pairs={{0,5},{1,4},{2,7},{3,6},{4,1},{5,0},{6,3},{7,2},{8,13},{9,12},{10,... | collective-permute-start | bytes 294920 | tf_op jit(solution)/shard_map/ppermute | solution.py:43
  87.9 8.8 %collective-permute-start.16 = (bf16[3,2,32,128]{3,2,1,0:T(8,128)(2,1)S(1)}, bf16[3,2,32,128]{3,2,1,0:T(8,128)(2,1)S(1)}, u32[]{:S(2)}, u32[]{:S(2)}) collective-permute-start(bf16[3,2,32,128]{3,2,1,0:T(8,128)(2,1)S(1)} %dynamic-slice_bitcast_fusion), channel_id=1, source_target_pairs={{0,64},{1,65},{2,66},{3,67},{4,68},{5,69},{6,70},{7,71},{8,72},{9,... | collective-permute-start | bytes 147464 | tf_op jit(solution)/shard_map/ppermute | solution.py:43
  96.8 5.2 %collective-permute-start.19 = (bf16[192,128]{1,0:T(8,128)(2,1)S(1)}, bf16[192,128]{1,0:T(8,128)(2,1)S(1)}, u32[]{:S(2)}, u32[]{:S(2)}) collective-permute-start(bf16[192,128]{1,0:T(8,128)(2,1)S(1)} %bitcast.28), channel_id=1, source_target_pairs={{0,48},{1,49},{2,50},{3,51},{4,52},{5,53},{6,54},{7,55},{8,56},{9,... | collective-permute-start | bytes 147464 | tf_op jit(solution)/shard_map/ppermute | solution.py:43
  104.4 5.7 %collective-permute-start.22 = (bf16[768,128]{1,0:T(8,128)(2,1)S(1)}, bf16[768,128]{1,0:T(8,128)(2,1)}, u32[]{:S(2)}, u32[]{:S(2)}) collective-permute-start(bf16[768,128]{1,0:T(8,128)(2,1)S(1)} %pad_maximum_fusion.1.x0), channel_id=1, source_target_pairs={{0,5},{1,4},{2,7},{3,6},{4,1},{5,0},{6,3},{7,2},{8,13},{9,12},{10,... | collective-permute-start | bytes 589832 | tf_op jit(solution)/shard_map/ppermute | solution.py:43
  104.6 6.1 %collective-permute-start.21 = (bf16[768,128]{1,0:T(8,128)(2,1)S(1)}, bf16[768,128]{1,0:T(8,128)(2,1)}, u32[]{:S(2)}, u32[]{:S(2)}) collective-permute-start(bf16[768,128]{1,0:T(8,128)(2,1)S(1)} %pad_maximum_fusion.1.x0), channel_id=1, source_target_pairs={{0,4},{1,5},{2,6},{3,7},{4,0},{5,1},{6,2},{7,3},{8,12},{9,13},{10,... | collective-permute-start | bytes 589832 | tf_op jit(solution)/shard_map/ppermute | solution.py:43
  105.4 6.8 %collective-permute-start.20 = (bf16[768,128]{1,0:T(8,128)(2,1)S(1)}, bf16[768,128]{1,0:T(8,128)(2,1)}, u32[]{:S(2)}, u32[]{:S(2)}) collective-permute-start(bf16[768,128]{1,0:T(8,128)(2,1)S(1)} %pad_maximum_fusion.1.x0), channel_id=1, source_target_pairs={{0,1},{1,0},{2,3},{3,2},{4,5},{5,4},{6,7},{7,6},{8,9},{9,8},{10,11... | collective-permute-start | bytes 589832 | tf_op jit(solution)/shard_map/ppermute | solution.py:43
  116.1 5.2 %collective-permute-start.23 = (f32[3,2,32,128]{3,2,1,0:T(8,128)S(1)}, f32[3,2,32,128]{3,2,1,0:T(8,128)S(1)}, u32[]{:S(2)}, u32[]{:S(2)}) collective-permute-start(f32[3,2,32,128]{3,2,1,0:T(8,128)S(1)} %get-tuple-element.34), channel_id=1, source_target_pairs={{0,3},{1,2},{2,1},{3,0},{4,7},{5,6},{6,5},{7,4},{8,11},{9,10},{10,... | collective-permute-start | bytes 294920 | tf_op jit(solution)/shard_map/ppermute | solution.py:43
  121.3 6.8 %collective-permute-start.25 = (f32[3,2,32,128]{3,2,1,0:T(8,128)S(1)}, f32[3,2,32,128]{3,2,1,0:T(8,128)S(1)}, u32[]{:S(2)}, u32[]{:S(2)}) collective-permute-start(f32[3,2,32,128]{3,2,1,0:T(8,128)S(1)} %get-tuple-element.36), channel_id=1, source_target_pairs={{0,15},{1,14},{2,13},{3,12},{4,11},{5,10},{6,9},{7,8},{8,7},{9,6},... | collective-permute-start | bytes 294920 | tf_op jit(solution)/shard_map/ppermute | solution.py:43
  128.1 5.4 %collective-permute-start.26 = (bf16[3,2,32,128]{3,2,1,0:T(8,128)(2,1)S(1)}, bf16[3,2,32,128]{3,2,1,0:T(8,128)(2,1)S(1)}, u32[]{:S(2)}, u32[]{:S(2)}) collective-permute-start(bf16[3,2,32,128]{3,2,1,0:T(8,128)(2,1)S(1)} %fusion.2), channel_id=1, source_target_pairs={{0,160},{1,161},{2,162},{3,163},{4,164},{5,165},{6,166},{7,167},{8... | collective-permute-start | bytes 147464 | tf_op jit(solution)/shard_map/ppermute | solution.py:43
  139.4 8.0 %collective-permute-start.32 = (bf16[768,128]{1,0:T(8,128)(2,1)S(1)}, bf16[768,128]{1,0:T(8,128)(2,1)S(1)}, u32[]{:S(2)}, u32[]{:S(2)}) collective-permute-start(bf16[768,128]{1,0:T(8,128)(2,1)S(1)} %pad_maximum_fusion.2.x0), channel_id=1, source_target_pairs={{0,15},{1,14},{2,13},{3,12},{4,11},{5,10},{6,9},{7,8},{8,7},{9,6},... | collective-permute-start | bytes 589832 | tf_op jit(solution)/shard_map/ppermute | solution.py:43
  140.5 6.9 %collective-permute-start.31 = (bf16[768,128]{1,0:T(8,128)(2,1)S(1)}, bf16[768,128]{1,0:T(8,128)(2,1)S(1)}, u32[]{:S(2)}, u32[]{:S(2)}) collective-permute-start(bf16[768,128]{1,0:T(8,128)(2,1)S(1)} %pad_maximum_fusion.2.x0), channel_id=1, source_target_pairs={{0,12},{1,13},{2,14},{3,15},{4,8},{5,9},{6,10},{7,11},{8,4},{9,5},... | collective-permute-start | bytes 589832 | tf_op jit(solution)/shard_map/ppermute | solution.py:43
  141.9 7.4 %collective-permute-start.30 = (bf16[768,128]{1,0:T(8,128)(2,1)S(1)}, bf16[768,128]{1,0:T(8,128)(2,1)S(1)}, u32[]{:S(2)}, u32[]{:S(2)}) collective-permute-start(bf16[768,128]{1,0:T(8,128)(2,1)S(1)} %pad_maximum_fusion.2.x0), channel_id=1, source_target_pairs={{0,3},{1,2},{2,1},{3,0},{4,7},{5,6},{6,5},{7,4},{8,11},{9,10},{10,... | collective-permute-start | bytes 589832 | tf_op jit(solution)/shard_map/ppermute | solution.py:43
  153.5 5.7 %collective-permute-start.35 = (f32[3,2,32,128]{3,2,1,0:T(8,128)S(1)}, f32[3,2,32,128]{3,2,1,0:T(8,128)S(1)}, u32[]{:S(2)}, u32[]{:S(2)}) collective-permute-start(f32[3,2,32,128]{3,2,1,0:T(8,128)S(1)} %get-tuple-element.40), channel_id=1, source_target_pairs={{0,5},{1,4},{2,7},{3,6},{4,1},{5,0},{6,3},{7,2},{8,13},{9,12},{10,... | collective-permute-start | bytes 294920 | tf_op jit(solution)/shard_map/ppermute | solution.py:43
  165.1 7.6 %collective-permute-start.41 = (bf16[768,128]{1,0:T(8,128)(2,1)S(1)}, bf16[768,128]{1,0:T(8,128)(2,1)S(1)}, u32[]{:S(2)}, u32[]{:S(2)}) collective-permute-start(bf16[768,128]{1,0:T(8,128)(2,1)S(1)} %pad_maximum_fusion.3.x0), channel_id=1, source_target_pairs={{0,5},{1,4},{2,7},{3,6},{4,1},{5,0},{6,3},{7,2},{8,13},{9,12},{10,... | collective-permute-start | bytes 589832 | tf_op jit(solution)/shard_map/ppermute | solution.py:43
  166.2 7.5 %collective-permute-start.40 = (bf16[768,128]{1,0:T(8,128)(2,1)S(1)}, bf16[768,128]{1,0:T(8,128)(2,1)S(1)}, u32[]{:S(2)}, u32[]{:S(2)}) collective-permute-start(bf16[768,128]{1,0:T(8,128)(2,1)S(1)} %pad_maximum_fusion.3.x0), channel_id=1, source_target_pairs={{0,4},{1,5},{2,6},{3,7},{4,0},{5,1},{6,2},{7,3},{8,12},{9,13},{10,... | collective-permute-start | bytes 589832 | tf_op jit(solution)/shard_map/ppermute | solution.py:43
  166.4 7.4 %collective-permute-start.39 = (bf16[768,128]{1,0:T(8,128)(2,1)S(1)}, bf16[768,128]{1,0:T(8,128)(2,1)S(1)}, u32[]{:S(2)}, u32[]{:S(2)}) collective-permute-start(bf16[768,128]{1,0:T(8,128)(2,1)S(1)} %pad_maximum_fusion.3.x0), channel_id=1, source_target_pairs={{0,1},{1,0},{2,3},{3,2},{4,5},{5,4},{6,7},{7,6},{8,9},{9,8},{10,11... | collective-permute-start | bytes 589832 | tf_op jit(solution)/shard_map/ppermute | solution.py:43
  178.1 5.1 %collective-permute-start.42 = (f32[3,2,32,128]{3,2,1,0:T(8,128)}, f32[3,2,32,128]{3,2,1,0:T(8,128)S(1)}, u32[]{:S(2)}, u32[]{:S(2)}) collective-permute-start(f32[3,2,32,128]{3,2,1,0:T(8,128)} %get-tuple-element.42), channel_id=1, source_target_pairs={{0,3},{1,2},{2,1},{3,0},{4,7},{5,6},{6,5},{7,4},{8,11},{9,10},{10,... | collective-permute-start | bytes 294920 | tf_op jit(solution)/shard_map/ppermute | solution.py:43
  179.7 6.8 %collective-permute-start.44 = (f32[3,2,32,128]{3,2,1,0:T(8,128)S(1)}, f32[3,2,32,128]{3,2,1,0:T(8,128)S(1)}, u32[]{:S(2)}, u32[]{:S(2)}) collective-permute-start(f32[3,2,32,128]{3,2,1,0:T(8,128)S(1)} %get-tuple-element.44), channel_id=1, source_target_pairs={{0,15},{1,14},{2,13},{3,12},{4,11},{5,10},{6,9},{7,8},{8,7},{9,6},... | collective-permute-start | bytes 294920 | tf_op jit(solution)/shard_map/ppermute | solution.py:43
  187.4 19.2 %collective-permute-start.45 = (bf16[3,2,32,128]{3,2,1,0:T(8,128)(2,1)S(1)}, bf16[3,2,32,128]{3,2,1,0:T(8,128)(2,1)S(1)}, u32[]{:S(2)}, u32[]{:S(2)}) collective-permute-start(bf16[3,2,32,128]{3,2,1,0:T(8,128)(2,1)S(1)} %get-tuple-element.45), channel_id=1, source_target_pairs={{0,64},{1,65},{2,66},{3,67},{4,68},{5,69},{6,70},{7,71},{8,72},{9,... | collective-permute-start | bytes 147464 | tf_op jit(solution)/shard_map/ppermute | solution.py:43
  (26 other events, 216.9 us)
